TPU v7x, 32 devices: a whole 2x2x4 slice. The times are simulated.
32 devices in a mesh: dp: 8 (over z, core), tp: 4 (over y, x).
Axes of the slice: x: 2, y: 2, z: 4, core: 2. Of those that a mesh axis runs over, the one named last changes fastest.
Arguments:
- x_in: bfloat16 [8192, 2048], P(('dp', 'tp')), may hold values from -6 to 6
- norm_gain: float32 [2048], replicated, may hold values from 0.5 to 1.5
- w_z: bfloat16 [2048, 4096], P(None, 'tp'), may hold values from -0.125 to 0.125
- w_x: bfloat16 [2048, 4096], P(None, 'tp'), may hold values from -0.125 to 0.125
- w_b: bfloat16 [2048, 128], P(None, 'tp'), may hold values from -0.125 to 0.125
- w_c: bfloat16 [2048, 128], P(None, 'tp'), may hold values from -0.125 to 0.125
- w_dt: bfloat16 [2048, 64], P(None, 'tp'), may hold values from -0.125 to 0.125
- conv_w: float32 [4352, 4], replicated, may hold values from -3 to 3
- conv_b: float32 [4352], replicated, may hold values from -3 to 3
- dt_bias: float32 [64], replicated, may hold values from -6 to -2
- a_log: float32 [64], replicated, may hold values from -2.5 to 0.5
- d_skip: float32 [64], replicated, may hold values from 0.5 to 1.5
- gate_gain: float32 [4096], replicated, may hold values from 0.5 to 1.5
- w_out: bfloat16 [4096, 2048], P('tp'), may hold values from -0.09375 to 0.09375
- doc_lens: int32 [8, 8], P('dp'), may hold values from 1 to 512, 1024 in all within a row
- d_out: bfloat16 [8192, 2048], P(('dp', 'tp')), may hold values from -6 to 6
Outputs:
- block_out: bfloat16 [8192, 2048], P(('dp', 'tp'))
- grad_x: float32 [8192, 2048], P(('dp', 'tp'))
- grad_norm_gain: float32 [2048], replicated
- grad_w_z: float32 [2048, 4096], P('dp', 'tp')
- grad_w_x: float32 [2048, 4096], P('dp', 'tp')
- grad_w_b: float32 [2048, 128], P('dp', 'tp')
- grad_w_c: float32 [2048, 128], P('dp', 'tp')
- grad_w_dt: float32 [2048, 64], P('dp', 'tp')
- grad_conv_w: float32 [4352, 4], replicated
- grad_conv_b: float32 [4352], replicated
- grad_dt_bias: float32 [64], replicated
- grad_a_log: float32 [64], replicated
- grad_d_skip: float32 [64], replicated
- grad_gate_gain: float32 [4096], replicated
- grad_w_out: float32 [4096, 2048], P('tp', 'dp')
Inputs may be any that keep to these rules, and one draw needn't show every extreme that they name: `doc_lens`: each row gives, in order, the lengths of the 8 documents packed into one sequence of 1024 tokens; a row sums to 1024 and its longest document has exactly 512 tokens.
All inputs are finite; a program needn't handle non-finite values.
Results may differ from a plain program's by a relative error of at most 0.012.
Values may be sent and summed in bfloat16 or wider, within the bound.
A program may use at most 256 MiB of HBM per device.

v0:
```python
import jax
import jax.numpy as jnp
from jax import lax
from jax.sharding import PartitionSpec as P

EPSILON = 1e-05
HIGHEST = lax.Precision.HIGHEST


def entering_2(array, axis, combine, identity, reverse):
    count, index = (lax.axis_size(axis), lax.axis_index(axis))
    everything = jax.tree.map(lambda part: lax.all_gather(part, axis), array)
    start = jax.tree.map(
        lambda part, zero: jnp.broadcast_to(jnp.asarray(zero, part.dtype), part.shape),
        array,
        identity,
    )

    def lap(k, before):
        at = count - 1 - k if reverse else k
        reached = at > index if reverse else at < index
        new = combine(before, jax.tree.map(lambda part: part[at], everything))
        return jax.tree.map(lambda a, b: jnp.where(reached, a, b), new, before)

    return lax.fori_loop(0, count, lap, start)


def span_parts(log_decay, segments, segment_prev):
    cumulative = jnp.cumsum(log_decay, axis=0)
    inward = jnp.exp(cumulative) * (segments == segment_prev).astype(jnp.float32)[:, None]
    carried = jnp.exp(cumulative[-1]) * (segments[-1] == segment_prev).astype(jnp.float32)
    return (cumulative, inward, carried)


def span_pass(state, values, b_rows, c_rows, log_decay, steps_dt, segments, segment_prev):
    cumulative, inward, carried = span_parts(log_decay, segments, segment_prev)
    length = segments.shape[0]
    order = jnp.arange(length, dtype=jnp.int32)
    same = (segments[:, None] == segments[None, :]) & (order[:, None] >= order[None, :])
    spread = cumulative[:, None, :] - cumulative[None, :, :]
    decays = jnp.exp(jnp.where(same[:, :, None], spread, -1e30))
    scores = jnp.dot(c_rows, b_rows.T, precision=HIGHEST)
    mixing = decays * scores[:, :, None] * steps_dt[None, :, :]
    output = jnp.einsum("tsh,shp->thp", mixing, values, precision=HIGHEST)
    output = (
        output + jnp.einsum("tn,hpn->thp", c_rows, state, precision=HIGHEST) * inward[:, :, None]
    )
    tail_same = segments == segments[-1]
    tail = (
        jnp.exp(jnp.where(tail_same[:, None], cumulative[-1][None, :] - cumulative, -1e30))
        * steps_dt
    )
    weighted = tail[:, :, None] * values
    state_out = carried[:, None, None] * state + jnp.einsum(
        "shp,sn->hpn", weighted, b_rows, precision=HIGHEST
    )
    return (output, state_out, carried)


def in_norm(values, gain):
    return (
        values
        * lax.rsqrt(jnp.mean(values * values, axis=-1, keepdims=True) + EPSILON)
        * gain[None, :]
    )


def combine(earlier, later):
    return (earlier[0] * later[0], later[0][:, None, None] * earlier[1] + later[1])


def body(
    x_in,
    norm_gain,
    w_z,
    w_x,
    w_b,
    w_c,
    w_dt,
    conv_w,
    conv_b,
    dt_bias,
    a_log,
    d_skip,
    gate_gain,
    w_out,
    doc_lens,
    d_out,
):
    tp_count = lax.axis_size("tp")
    tp_rank = lax.axis_index("tp")
    dev_rows = x_in.shape[0]
    group_rows = dev_rows * tp_count
    head_count = dt_bias.shape[0]
    inner_width = gate_gain.shape[0]
    head_size = inner_width // head_count
    state_size = (conv_w.shape[0] - inner_width) // 2
    rim_rows = conv_w.shape[1] - 1
    col_widths = [w_z.shape[1], w_x.shape[1], w_b.shape[1], w_c.shape[1], w_dt.shape[1]]
    col_edges = [0]
    for col_width in col_widths:
        col_edges.append(col_edges[-1] + col_width)
    total_cols = col_edges[-1]
    contract_first = (((0,), (0,)), ((), ()))
    contract_last = (((1,), (1,)), ((), ()))
    lengths = doc_lens[0]
    doc_starts = jnp.cumsum(lengths) - lengths
    positions = tp_rank * dev_rows - rim_rows + jnp.arange(dev_rows + rim_rows, dtype=jnp.int32)
    seg_ext = jnp.sum((positions[:, None] >= doc_starts[None, :]).astype(jnp.int32), axis=1)
    seg_own = seg_ext[rim_rows:]
    seg_before = [seg_ext[rim_rows - 1]]
    x_float = x_in.astype(jnp.float32)
    normed = in_norm(x_float, norm_gain).astype(jnp.bfloat16)
    w_joined = jnp.concatenate([w_z, w_x, w_b, w_c, w_dt], axis=1)
    gathered = lax.all_gather(normed, "tp", axis=0, tiled=True)
    projected = jnp.dot(gathered, w_joined, preferred_element_type=jnp.float32).astype(jnp.bfloat16)
    padded = jnp.concatenate([jnp.zeros((rim_rows, total_cols), jnp.bfloat16), projected], axis=0)
    rims = padded[:group_rows].reshape(tp_count, dev_rows, total_cols)[:, :rim_rows]
    blocks = jnp.concatenate([rims, projected.reshape(tp_count, dev_rows, total_cols)], axis=1)
    arrived = lax.all_to_all(blocks, "tp", split_axis=0, concat_axis=2, tiled=True).reshape(
        dev_rows + rim_rows, tp_count, total_cols
    )

    def columns(source, which):
        return source[:, :, col_edges[which] : col_edges[which + 1]].reshape(source.shape[0], -1)

    gate_in = columns(arrived[rim_rows:], 0).astype(jnp.float32)
    conv_in = jnp.concatenate(
        [columns(arrived, 1), columns(arrived, 2), columns(arrived, 3)], axis=1
    ).astype(jnp.float32)
    dt_in = columns(arrived[rim_rows:], 4).astype(jnp.float32)

    def prepare(conv_in, dt_in, conv_w, conv_b, dt_bias, a_log):
        summed = jnp.zeros((dev_rows, conv_in.shape[1]), jnp.float32) + conv_b[None, :]
        for kernel_tap in range(conv_w.shape[1]):
            match = (seg_ext[kernel_tap : kernel_tap + dev_rows] == seg_own).astype(jnp.float32)
            summed = (
                summed
                + conv_w[:, kernel_tap][None, :]
                * conv_in[kernel_tap : kernel_tap + dev_rows]
                * match[:, None]
            )
        active = jax.nn.silu(summed)
        values = active[:, :inner_width].reshape(dev_rows, head_count, head_size)
        b_rows = active[:, inner_width : inner_width + state_size]
        c_rows = active[:, inner_width + state_size :]
        steps_dt = jax.nn.softplus(dt_in + dt_bias[None, :])
        log_decay = -steps_dt * jnp.exp(a_log)[None, :]
        return (values, b_rows, c_rows, log_decay, steps_dt)

    prepared, prepare_back = jax.vjp(prepare, conv_in, dt_in, conv_w, conv_b, dt_bias, a_log)
    values, b_rows, c_rows, log_decay, steps_dt = prepared

    def ssd_local(values, b_rows, c_rows, log_decay, steps_dt):
        state = jnp.zeros((head_count, head_size, state_size), jnp.float32)
        carried_all = jnp.ones((head_count,), jnp.float32)
        output, state, carried = span_pass(
            state, values, b_rows, c_rows, log_decay, steps_dt, seg_own, seg_before[0]
        )
        outputs = [output]
        carried_all = carried_all * carried
        return (jnp.concatenate(outputs, axis=0), carried_all, state)

    def entering(state_in, c_rows, log_decay):
        decay = jnp.ones((head_count,), jnp.float32)
        cumulative, inward, carried = span_parts(log_decay, seg_own, seg_before[0])
        reached = jnp.einsum(
            "tn,hpn->thp", c_rows, decay[:, None, None] * state_in, precision=HIGHEST
        )
        outputs = [reached * inward[:, :, None]]
        return jnp.concatenate(outputs, axis=0)

    identity = (
        jnp.ones((head_count,), jnp.float32),
        jnp.zeros((head_count, head_size, state_size), jnp.float32),
    )
    local_parts, ssd_back = jax.vjp(ssd_local, values, b_rows, c_rows, log_decay, steps_dt)
    local_out, carried_dev, state_dev = local_parts
    chained = entering_2((carried_dev, state_dev), "tp", combine, identity, False)
    state_in = chained[1]
    extra_out, entering_back = jax.vjp(entering, state_in, c_rows, log_decay)
    ssd_out = local_out + extra_out

    def gated(ssd_out, values, gate_in, d_skip, gate_gain):
        mixed_heads = ssd_out + d_skip[None, :, None] * values
        flat = mixed_heads.reshape(dev_rows, inner_width)
        gated_rows = flat * jax.nn.silu(gate_in)
        scale = lax.rsqrt(jnp.mean(gated_rows * gated_rows, axis=-1, keepdims=True) + EPSILON)
        return gated_rows * scale * gate_gain[None, :]

    normal_out, gated_back = jax.vjp(gated, ssd_out, values, gate_in, d_skip, gate_gain)
    rounded = normal_out.astype(jnp.bfloat16)
    by_heads = lax.all_to_all(rounded, "tp", split_axis=1, concat_axis=0, tiled=True)
    branch_out = lax.psum_scatter(
        jnp.dot(by_heads, w_out, preferred_element_type=jnp.float32),
        "tp",
        scatter_dimension=0,
        tiled=True,
    )
    block_out = (x_float + branch_out).astype(jnp.bfloat16)
    grad_gathered = lax.all_gather(d_out, "tp", axis=0, tiled=True)
    grad_heads = lax.dot_general(
        grad_gathered, w_out, contract_last, preferred_element_type=jnp.float32
    ).astype(jnp.bfloat16)
    grad_normal = lax.all_to_all(grad_heads, "tp", split_axis=0, concat_axis=1, tiled=True)
    grad_ssd, grad_values_a, grad_gate_in, grad_skip, grad_gate_gain = gated_back(
        grad_normal.astype(jnp.float32)
    )
    grad_state_in, grad_c_a, grad_decay_a = entering_back(grad_ssd)
    chained_back = entering_2((carried_dev, grad_state_in), "tp", combine, identity, True)
    grad_state_dev = chained_back[1]
    grad_carried = jnp.sum(grad_state_dev * state_in, axis=(1, 2))
    grad_values_b, grad_b, grad_c_b, grad_decay_b, grad_dt = ssd_back(
        (grad_ssd, grad_carried, grad_state_dev)
    )
    grad_conv_in, grad_dt_in, grad_conv_w, grad_conv_b, grad_dt_bias, grad_a_log = prepare_back(
        (
            grad_values_a + grad_values_b,
            grad_b,
            grad_c_a + grad_c_b,
            grad_decay_a + grad_decay_b,
            grad_dt,
        )
    )

    def split_heads(array):
        return array.reshape(array.shape[0], tp_count, -1)

    grad_gate_full = jnp.concatenate(
        [jnp.zeros((rim_rows, inner_width), jnp.float32), grad_gate_in], axis=0
    )
    grad_dt_full = jnp.concatenate(
        [jnp.zeros((rim_rows, head_count), jnp.float32), grad_dt_in], axis=0
    )
    pieces = [
        split_heads(grad_gate_full),
        split_heads(grad_conv_in[:, :inner_width]),
        split_heads(grad_conv_in[:, inner_width : inner_width + state_size]),
        split_heads(grad_conv_in[:, inner_width + state_size :]),
        split_heads(grad_dt_full),
    ]
    outgoing = jnp.concatenate(pieces, axis=2).reshape(
        1, dev_rows + rim_rows, tp_count * total_cols
    )
    returned = lax.all_to_all(outgoing, "tp", split_axis=2, concat_axis=0, tiled=True)
    main_rows = returned[:, rim_rows:]
    main_rows = main_rows.at[:-1, dev_rows - rim_rows :].add(returned[1:, :rim_rows])
    grad_projected = main_rows.reshape(group_rows, total_cols).astype(jnp.bfloat16)
    grad_normed = lax.psum_scatter(
        lax.dot_general(
            grad_projected, w_joined, contract_last, preferred_element_type=jnp.float32
        ),
        "tp",
        scatter_dimension=0,
        tiled=True,
    )
    _, norm_back = jax.vjp(in_norm, x_float, norm_gain)
    grad_x_norm, grad_norm_gain = norm_back(grad_normed)
    grad_x = d_out.astype(jnp.float32) + grad_x_norm
    in_part = lax.dot_general(
        gathered, grad_projected, contract_first, preferred_element_type=jnp.float32
    )
    weight_grads = lax.psum_scatter(
        jnp.concatenate(
            [
                in_part,
                lax.dot_general(
                    grad_gathered, by_heads, contract_first, preferred_element_type=jnp.float32
                ),
            ],
            axis=1,
        ),
        "dp",
        scatter_dimension=0,
        tiled=True,
    )
    grad_w_z = weight_grads[:, col_edges[0] : col_edges[1]]
    grad_w_x = weight_grads[:, col_edges[1] : col_edges[2]]
    grad_w_b = weight_grads[:, col_edges[2] : col_edges[3]]
    grad_w_c = weight_grads[:, col_edges[3] : col_edges[4]]
    grad_w_dt = weight_grads[:, col_edges[4] : col_edges[5]]
    grad_w_out = weight_grads[:, total_cols:].T
    summed_small = lax.psum(
        (
            grad_norm_gain,
            grad_conv_w,
            grad_conv_b,
            grad_dt_bias,
            grad_a_log,
            grad_skip,
            grad_gate_gain,
        ),
        ("dp", "tp"),
    )
    return (
        block_out,
        grad_x,
        summed_small[0],
        grad_w_z,
        grad_w_x,
        grad_w_b,
        grad_w_c,
        grad_w_dt,
        summed_small[1],
        summed_small[2],
        summed_small[3],
        summed_small[4],
        summed_small[5],
        summed_small[6],
        grad_w_out,
    )


def solution(mesh):
    placed = (
        P(("dp", "tp"), None),
        P(),
        P(None, "tp"),
        P(None, "tp"),
        P(None, "tp"),
        P(None, "tp"),
        P(None, "tp"),
        P(),
        P(),
        P(),
        P(),
        P(),
        P(),
        P("tp", None),
        P("dp", None),
        P(("dp", "tp"), None),
    )
    return jax.shard_map(
        body,
        mesh=mesh,
        in_specs=placed,
        out_specs=(
            P(("dp", "tp"), None),
            P(("dp", "tp"), None),
            P(),
            P("dp", "tp"),
            P("dp", "tp"),
            P("dp", "tp"),
            P("dp", "tp"),
            P("dp", "tp"),
            P(),
            P(),
            P(),
            P(),
            P(),
            P(),
            P("tp", "dp"),
        ),
        check_vma=False,
    )
```

profile of v0, /device:TPU:1, one launch (start us, length us, event | category | flops | bytes accessed | tf_op | source)
XLA Modules:
  0.0 1443.4 jit_solution(17318158812077434221)
XLA Ops:
  12.3 14.3 concatenate.29
  26.6 39.8 %all-gather.8.cloned.1.call-done = bf16[1024,2048]{1,0:T(8,128)(2,1)} async-done(((bf16[256,2048]{1,0:T(8,128)(2,1)}), bf16[1024,2048]{1,0:T(8,128)(2,1)}) %all-gather.8.cloned.1.call-update) | async-done | bytes 4194320 | tf_op jit(solution)/shard_map/all_gather | solution.py:115
  66.3 13.6 convolution_convert_fusion
  117.4 60.6 %all-to-all-done = bf16[4,259,2128]{2,1,0:T(8,128)(2,1)} async-done(((bf16[4,259,2128]{2,1,0:T(8,128)(2,1)}), bf16[4,259,2128]{2,1,0:T(8,128)(2,1)}, u32[]{:S(2)}, u32[]{:S(2)}) %all-to-all-start) | async-done | bytes 4409248 | tf_op jit(solution)/shard_map/all_to_all | solution.py:120
  240.8 43.3 %all-to-all-done.2 = bf16[4,256,1024]{1,2,0:T(8,128)(2,1)} async-done(((bf16[4,256,1024]{1,2,0:T(8,128)(2,1)}), bf16[4,256,1024]{1,2,0:T(8,128)(2,1)}, u32[]{:S(2)}, u32[]{:S(2)}) %all-to-all-start.2) | async-done | bytes 2097184 | tf_op jit(solution)/shard_map/all_to_all | solution.py:205
  305.8 32.7 %all-gather.12.cloned.1.call-done = f32[256,64,128]{2,1,0:T(8,128)} async-done(((f32[64,64,128]{2,1,0:T(8,128)}), f32[256,64,128]{2,1,0:T(8,128)}) %all-gather.12.cloned.1.call-update) | async-done | bytes 8388624 | tf_op jit(solution)/shard_map/all_gather | solution.py:12
  351.5 23.6 %multiply_reduce_fusion.11 = (f32[256]{0:T(256)S(1)}, f32[256,64,64]{0,2,1:T(8,128)S(1)}, f32[256,64,64]{0,2,1:T(8,128)}) fusion(f32[256,64,64]{0,2,1:T(8,128)} %bitcast.311, f32[256,64,64]{0,2,1:T(8,128)S(1)} %bitcast.299, f32[64]{0:T(128)S(1)} %copy-done.73, f32[256,64,64]{0,2,1:T(8,128)S(1)} %fusion.100, f32[256,64,64]{0,2,1:T(8,128)} %fusion.92, ...), kind=kOutput, calls=%fused_computation.87 | convolution fusion | flops 3251633920 | bytes 25691392 | tf_op jit(solution)/shard_map/jvp(tsh,shp->thp)/dot_general | solution.py:44
  426.6 26.2 %fusion.10 = (f32[256,64]{0,1:T(8,128)S(1)}, f32[256,64]{0,1:T(8,128)S(1)}, f32[256,64]{0,1:T(8,128)}, f32[256,256]{1,0:T(8,128)S(1)}) fusion(f32[256,64]{0,1:T(8,128)S(1)} %copy-done.43, f32[256,256]{1,0:T(8,128)S(1)} %copy-done.23, f32[256,64]{0,1:T(8,128)S(1)} %bitcast_bitcast_fusion.1, pred[256,256]{1,0:T(8,128)(4,1)S(1)} %fusion.95, ...), kind=kOutput, calls=%fused_computation.18 | convolution fusion | flops 3275636736 | bytes 9306112 | tf_op jit(solution)/shard_map/transpose(jvp(tsh,shp->thp))/dot_general | solution.py:44
  454.0 24.7 %all-gather.14.cloned.1.call-done = f32[256,64,128]{2,1,0:T(8,128)} async-done(((f32[64,64,128]{2,1,0:T(8,128)}), f32[256,64,128]{2,1,0:T(8,128)}) %all-gather.14.cloned.1.call-update) | async-done | bytes 8388624 | tf_op jit(solution)/shard_map/all_gather | solution.py:12
  478.7 14.9 %while.32 = (s32[]{:T(128)}, f32[64,64,128]{2,1,0:T(8,128)}, s32[]{:T(128)}, f32[4,64]{1,0:T(4,128)S(1)}, f32[4,64,64,128]{3,2,1,0:T(8,128)}, /*index=5*/s32[]{:T(128)}, s32[]{:T(128)}, s32[]{:T(128)}, s32[]{:T(128)}) while((s32[]{:T(128)}, f32[64,64,128]{2,1,0:T(8,128)}, s32[]{:T(128)}, f32[4,64]{1,0:T(4,128)S(1)}, ...), condition=%wide.region_12.13_spmd.clone, body=%wide.region_11.12_spmd.clone.sunk | while | flops 2097160 | bytes 6292391 | solution.py:25
  510.5 15.7 %fusion.31 = f32[256,64,64]{0,2,1:T(8,128)} fusion(f32[256,64,64]{0,2,1:T(8,128)S(1)} %get-tuple-element.469, f32[256,64,64]{0,2,1:T(8,128)S(1)} %copy-done.7, f32[64]{0:T(128)S(1)} %copy-done.73, f32[256,64]{0,1:T(8,128)S(1)} %get-tuple-element.456, f32[256,64]{0,1:T(8,128)S(1)} %copy-done.43, f32[256,256]{1,0:T(8,128)S(1)} %copy-done.24, ...), kind=kOutput, calls=%fused_computation.58 | convolution fusion | flops 3242196992 | bytes 13107456 | tf_op jit(solution)/shard_map/transpose(jvp(tsh,shp->thp))/dot_general | solution.py:44
  532.2 12.2 multiply_reduce_fusion.4
  572.4 15.8 %concatenate.35 = f32[259,4,2128]{2,1,0:T(4,128)} concatenate(f32[259,4,1024]{2,1,0:T(4,128)} %copy.193, f32[259,4,1024]{2,1,0:T(4,128)} %reshape.445, f32[259,4,32]{2,1,0:T(4,128)S(1)} %copy.194, f32[259,4,32]{2,1,0:T(4,128)S(1)} %copy.195, f32[259,4,16]{2,1,0:T(4,128)S(1)} %copy.196), dimensions={2} | concatenate | bytes 17636864 | tf_op jit(solution)/shard_map/concatenate | solution.py:242
  599.6 27.3 %copy.197 = f32[1,259,8512]{1,0,2:T(1,128)} copy(f32[1,259,8512]{2,1,0:T(8,128)} %reshape.454) | data formatting | bytes 17636864 | tf_op jit(solution)/shard_map/reshape | solution.py:242
  634.7 140.7 %all-to-all-done.3 = f32[1,259,8512]{1,0,2:T(1,128)} async-done(((f32[1,259,8512]{1,0,2:T(1,128)}), f32[1,259,8512]{1,0,2:T(1,128)}, u32[]{:S(2)}, u32[]{:S(2)}) %all-to-all-start.3) | async-done | bytes 8818464 | tf_op jit(solution)/shard_map/all_to_all | solution.py:245
  802.5 22.9 %scatter-add.4 = f32[4,256,2128]{1,2,0:T(8,128)} dynamic-update-slice(f32[4,256,2128]{1,2,0:T(8,128)} %copy-done.8, f32[3,3,2128]{1,2,0:T(8,128)S(1)} %add_select_fusion, s32[]{:T(128)} %bitcast.52, s32[]{:T(128)} %bitcast.53, s32[]{:T(128)} %constant.140.clone.1) | dynamic-update-slice | bytes 153220 | tf_op jit(solution)/shard_map/scatter-add | solution.py:247
  837.7 15.7 %fusion.148 = f32[1024,2048]{1,0:T(8,128)} fusion(bf16[1024,2128]{1,0:T(8,128)(2,1)} %bitcast.319, bf16[2048,2128]{1,0:T(8,128)(2,1)} %concatenate.29), kind=kOutput, calls=%fused_computation.237 | convolution fusion | flops 8925478912 | bytes 21463040 | tf_op jit(solution)/shard_map/dot_general | solution.py:250
  857.8 49.7 %all_to_all.62 = bf16[256,4,1024]{0,2,1:T(8,128)(2,1)S(1)} all-to-all(bf16[256,4,1024]{0,2,1:T(8,128)(2,1)S(1)} %fusion.48), channel_id=1, replica_groups=mesh['dp'=8,'tp'=4] {'tp'}, dimensions={1} | all-to-all | bytes 4194304 | tf_op jit(solution)/shard_map/all_to_all | solution.py:193
  931.3 12.9 fusion.149
  944.2 16.0 %pad_maximum_fusion = f32[2048,3152]{0,1:T(8,128)} fusion(f32[2048,1024]{0,1:T(8,128)} %convolution_bitcast_fusion, f32[2048,2128]{0,1:T(8,128)S(1)} %fusion.149), kind=kLoop, calls=%fused_computation.6 | loop fusion | flops 6455296 | bytes 51642368 | tf_op jit(solution)/shard_map/concatenate | solution.py:264
  965.7 41.9 %all-reduce.16 = (f32[2048]{0:T(1024)}, f32[4352]{0:T(1024)}, f32[64]{0:T(128)}, f32[64]{0:T(128)}, f32[64]{0:T(128)}, /*index=5*/f32[4096]{0:T(1024)}) all-reduce(f32[2048]{0:T(1024)S(1)} %get-tuple-element.395, f32[4352]{0:T(1024)S(1)} %copy-done.32, f32[64]{0:T(128)S(1)} %get-tuple-element.431, ...), channel_id=1, replica_groups=mesh['dp'=8,'tp'=4] {'dp','tp'}, use_global_device_ids=true, to_apply=%region_30.31 | all-reduce | flops 10688 | bytes 85504 | tf_op jit(solution)/shard_map/psum | solution.py:283
  1007.6 46.4 %reduce-scatter.4.cloned.1.call-done = f32[256,2048]{1,0:T(8,128)} async-done(((f32[1024,2048]{1,0:T(8,128)}), f32[256,2048]{1,0:T(8,128)}) %reduce-scatter.4.cloned.1.call-update) | async-done | bytes 2097168 | tf_op jit(solution)/shard_map/reduce_scatter | solution.py:194
  1058.3 249.3 %reduce-scatter.8.cloned.1.call-done = f32[256,3152]{0,1:T(8,128)} async-done(((f32[2048,3152]{0,1:T(8,128)}), f32[256,3152]{0,1:T(8,128)}) %reduce-scatter.8.cloned.1.call-update) | async-done | bytes 3227664 | tf_op jit(solution)/shard_map/reduce_scatter | solution.py:263
  1316.0 118.6 %all-reduce.19.cloned.1.call-done = f32[4352,4]{0,1:T(4,128)} async-done(((f32[4352,4]{0,1:T(4,128)}), f32[4352,4]{0,1:T(4,128)}) %all-reduce.19.cloned.1.call-update) | async-done | bytes 69648 | tf_op jit(solution)/shard_map/psum | solution.py:283
  (317 shorter events, 370.8 us)
Async XLA Ops:
  7.2 59.1 %all-gather.8.cloned.1.call-start = ((), (), s32[]{:S(2)}) async-start(), calls=%async_computation.7 | async-start | bytes 5242880 | tf_op jit(solution)/shard_map/all_gather | solution.py:115
  106.0 72.0 %all-to-all-start = ((bf16[4,259,2128]{2,1,0:T(8,128)(2,1)}), bf16[4,259,2128]{2,1,0:T(8,128)(2,1)}, u32[]{:S(2)}, u32[]{:S(2)}) async-start(bf16[4,259,2128]{2,1,0:T(8,128)(2,1)} %pad_maximum_fusion.1), calls=%async_computation | async-start | bytes 9191424 | tf_op jit(solution)/shard_map/all_to_all | solution.py:120
  111.1 114.3 %all-gather.10.cloned.1.call-start = ((), (), s32[]{:S(2)}) async-start(), calls=%async_computation.9 | async-start | bytes 5242880 | tf_op jit(solution)/shard_map/all_gather | solution.py:201
  111.8 226.7 %all-gather.12.cloned.1.call-start = ((), (), s32[]{:S(2)}) async-start(), calls=%async_computation.13 | async-start | bytes 10485760 | tf_op jit(solution)/shard_map/all_gather | solution.py:12
  112.4 80.9 %copy-start.68 = (f32[64]{0:T(128)}, f32[64]{0:T(128)S(1)}, u32[]{:S(2)}) copy-start(f32[64]{0:T(128)S(1)} %exp.58) | copy-start | bytes 772
  112.7 73.5 %copy-start.45 = (s32[259]{0:T(512)}, s32[259]{0:T(512)S(1)}, u32[]{:S(2)}) copy-start(s32[259]{0:T(512)S(1)} %convert_reduce_fusion) | copy-start | bytes 3112
  193.4 24.8 %copy-start.20 = (bf16[256,4,16]{0,2,1:T(8,128)(2,1)}, bf16[256,4,16]{0,2,1:T(8,128)(2,1)S(1)}, u32[]{:S(2)}) copy-start(bf16[256,4,16]{0,2,1:T(8,128)(2,1)S(1)} %slice.224) | copy-start | bytes 98308
  218.3 133.2 %copy-start.42 = (f32[256,64]{0,1:T(8,128)}, f32[256,64]{0,1:T(8,128)S(1)}, u32[]{:S(2)}) copy-start(f32[256,64]{0,1:T(8,128)S(1)} %get-tuple-element.457) | copy-start | bytes 196612
  236.0 48.2 %all-to-all-start.2 = ((bf16[4,256,1024]{1,2,0:T(8,128)(2,1)}), bf16[4,256,1024]{1,2,0:T(8,128)(2,1)}, u32[]{:S(2)}, u32[]{:S(2)}) async-start(bf16[4,256,1024]{1,2,0:T(8,128)(2,1)} %copy.184), calls=%async_computation.3 | async-start | bytes 4194304 | tf_op jit(solution)/shard_map/all_to_all | solution.py:205
  240.5 238.3 %all-gather.14.cloned.1.call-start = ((), (), s32[]{:S(2)}) async-start(), calls=%async_computation.14 | async-start | bytes 10485760 | tf_op jit(solution)/shard_map/all_gather | solution.py:12
  240.8 185.7 %copy-start.40 = (pred[256,256]{1,0:T(8,128)(4,1)}, pred[256,256]{1,0:T(8,128)(4,1)S(1)}, u32[]{:S(2)}) copy-start(pred[256,256]{1,0:T(8,128)(4,1)S(1)} %fusion.95) | copy-start | bytes 196612
  295.7 55.8 %copy-start.22 = (f32[256,256]{1,0:T(8,128)}, f32[256,256]{1,0:T(8,128)S(1)}, u32[]{:S(2)}) copy-start(f32[256,256]{1,0:T(8,128)S(1)} %fusion.106) | copy-start | bytes 786436
  351.5 23.7 %copy-start.16 = (f32[256,64,64]{0,2,1:T(8,128)}, f32[256,64,64]{0,2,1:T(8,128)S(1)}, u32[]{:S(2)}) copy-start(f32[256,64,64]{0,2,1:T(8,128)S(1)} %fusion.100) | copy-start | bytes 12582916
  351.5 23.6 %copy-start.11 = (f32[4,256,1024]{1,2,0:T(8,128)S(1)}, f32[4,256,1024]{1,2,0:T(8,128)}, u32[]{:S(2)}) copy-start(f32[4,256,1024]{1,2,0:T(8,128)} %convert_element_type.132) | copy-start | bytes 12582916
  375.1 18.6 %copy-start.47 = (f32[256]{0:T(256)}, f32[256]{0:T(256)S(1)}, u32[]{:S(2)}) copy-start(f32[256]{0:T(256)S(1)} %fusion.132) | copy-start | bytes 3076
  493.6 9.9 copy-start.4
  549.4 10.6 copy-start.44
  549.5 10.6 copy-start.69
  626.8 148.5 %all-to-all-start.3 = ((f32[1,259,8512]{1,0,2:T(1,128)}), f32[1,259,8512]{1,0,2:T(1,128)}, u32[]{:S(2)}, u32[]{:S(2)}) async-start(f32[1,259,8512]{1,0,2:T(1,128)} %copy.197), calls=%async_computation.4 | async-start | bytes 26148864 | tf_op jit(solution)/shard_map/all_to_all | solution.py:245
  633.3 329.9 %reduce-scatter.6.cloned.1.call-start = ((), (), s32[]{:S(2)}) async-start(), calls=%async_computation.10 | async-start | bytes 10485760 | tf_op jit(solution)/shard_map/reduce_scatter | solution.py:249
  853.5 200.5 %reduce-scatter.4.cloned.1.call-start = ((), (), s32[]{:S(2)}) async-start(), calls=%async_computation.8 | async-start | bytes 10485760 | tf_op jit(solution)/shard_map/reduce_scatter | solution.py:194
  920.6 387.0 %reduce-scatter.8.cloned.1.call-start = ((), (), s32[]{:S(2)}) async-start(), calls=%async_computation.11 | async-start | bytes 29048832 | tf_op jit(solution)/shard_map/reduce_scatter | solution.py:263
  960.3 474.2 %all-reduce.19.cloned.1.call-start = ((), (), s32[]{:S(2)}) async-start(), calls=%async_computation.12 | async-start | bytes 139264 | tf_op jit(solution)/shard_map/psum | solution.py:283
  963.3 90.7 %copy-start.18 = (f32[256,2048]{1,0:T(8,128)S(1)}, f32[256,2048]{1,0:T(8,128)}, u32[]{:S(2)}) copy-start(f32[256,2048]{1,0:T(8,128)} %reduce-scatter.6.cloned.1.call-done) | copy-start | bytes 6291460
  (63 other events, 266.6 us)
Sparse Core Ops, SparseCore 0:
  11.5 54.7 all-gather.7
  113.7 83.3 all-gather.9
  225.4 113.0 all-gather.11
  391.1 87.6 all-gather.13
  853.6 109.6 reduce-scatter.5
  966.5 87.4 reduce-scatter.3
  1056.3 251.1 reduce-scatter.7
  1314.7 119.8 all-reduce.18
where the time goes:
time: 1460 us; the launch traced here: 1440 us
  waiting for transfers between devices  758 us (52%)
  local copies, waits for them, and re-layouts  230 us (16%)
  matrix products  193 us (13%)
  other arithmetic  130 us (9%)
  blocking collectives  97.8 us (7%)
  between operations  17.1 us (1%)
  starting transfers between devices  16.9 us (1%)
    reduce_scatter x1, waiting for transfers between devices, body(): lax.psum_scatter(jnp.concatenate([in_part, lax.dot_general(grad_gathered,...  249 us
    all_to_all x1, waiting for transfers between devices, body(): lax.all_to_all(outgoing, 'tp', split_axis=2, concat_axis=0, tiled=True)  141 us
    psum x1, waiting for transfers between devices, body(): lax.psum((grad_norm_gain, grad_conv_w, grad_conv_b, grad_dt_bias, grad_a_...  119 us
    dot_general x3, matrix products, span_pass(): output = jnp.einsum('tsh,shp->thp', mixing, values, precision=HIGHEST)  65.4 us
    all_to_all x1, waiting for transfers between devices, body(): lax.all_to_all(blocks, 'tp', split_axis=0, concat_axis=2, tiled=True)  60.6 us
    all_gather x2, waiting for transfers between devices, entering_2(): everything = jax.tree.map(lambda part: lax.all_gather(part, axis), array)  57.4 us
    all_to_all x1, blocking collectives, body(): lax.all_to_all(rounded, 'tp', split_axis=1, concat_axis=0, tiled=True)  49.7 us
    reduce_scatter x1, waiting for transfers between devices, body(): lax.psum_scatter(jnp.dot(by_heads, w_out, preferred_element_type=jnp.floa...  46.4 us
  transfers between devices with their start and end apart: 11, of which 10 were waited for; matrix products, arithmetic and copies ran while one was open for 15% of the time, Pallas kernels for 0%

commit v1 on v0

--- a/solution.py
+++ b/solution.py
@@ -5,6 +5,12 @@
 
 EPSILON = 1e-05
 HIGHEST = lax.Precision.HIGHEST
+
+
+def swap_blocks(shard, axis, split, join):
+    cells = jnp.split(shard, lax.axis_size(axis), axis=split)
+    incoming = lax.all_to_all(jnp.stack(cells), axis, 0, 0)
+    return jnp.concatenate(incoming, axis=join)
 
 
 def entering_2(array, axis, combine, identity, reverse):
@@ -117,9 +123,7 @@
     padded = jnp.concatenate([jnp.zeros((rim_rows, total_cols), jnp.bfloat16), projected], axis=0)
     rims = padded[:group_rows].reshape(tp_count, dev_rows, total_cols)[:, :rim_rows]
     blocks = jnp.concatenate([rims, projected.reshape(tp_count, dev_rows, total_cols)], axis=1)
-    arrived = lax.all_to_all(blocks, "tp", split_axis=0, concat_axis=2, tiled=True).reshape(
-        dev_rows + rim_rows, tp_count, total_cols
-    )
+    arrived = swap_blocks(blocks, "tp", 0, 2).reshape(dev_rows + rim_rows, tp_count, total_cols)
 
     def columns(source, which):
         return source[:, :, col_edges[which] : col_edges[which + 1]].reshape(source.shape[0], -1)

time: 1460 us -> 1460 us (level)
  no operation moved by 1% of the time
where the time goes in v1:
time: 1460 us; the launch traced here: 1440 us
  waiting for transfers between devices  758 us (52%)
  local copies, waits for them, and re-layouts  230 us (16%)
  matrix products  193 us (13%)
  other arithmetic  131 us (9%)
  blocking collectives  97.8 us (7%)
  between operations  17.1 us (1%)
  starting transfers between devices  16.9 us (1%)
    reduce_scatter x1, waiting for transfers between devices, body(): lax.psum_scatter(jnp.concatenate([in_part, lax.dot_general(grad_gathered,...  249 us
    all_to_all x1, waiting for transfers between devices, body(): lax.all_to_all(outgoing, 'tp', split_axis=2, concat_axis=0, tiled=True)  141 us
    psum x1, waiting for transfers between devices, body(): lax.psum((grad_norm_gain, grad_conv_w, grad_conv_b, grad_dt_bias, grad_a_...  119 us
    dot_general x3, matrix products, span_pass(): output = jnp.einsum('tsh,shp->thp', mixing, values, precision=HIGHEST)  65.4 us
    all_to_all x1, waiting for transfers between devices, swap_blocks(): incoming = lax.all_to_all(jnp.stack(cells), axis, 0, 0)  60.6 us
    all_gather x2, waiting for transfers between devices, entering_2(): everything = jax.tree.map(lambda part: lax.all_gather(part, axis), array)  57.4 us
    all_to_all x1, blocking collectives, body(): lax.all_to_all(rounded, 'tp', split_axis=1, concat_axis=0, tiled=True)  49.7 us
    reduce_scatter x1, waiting for transfers between devices, body(): lax.psum_scatter(jnp.dot(by_heads, w_out, preferred_element_type=jnp.floa...  46.4 us
  transfers between devices with their start and end apart: 11, of which 10 were waited for; matrix products, arithmetic and copies ran while one was open for 15% of the time, Pallas kernels for 0%

profile of v1, /device:TPU:1, one launch (start us, length us, event | category | flops | bytes accessed | tf_op | source)
XLA Modules:
  0.0 1444.1 jit_solution(8761543569129856060)
XLA Ops:
  12.3 14.3 concatenate.29
  26.6 39.8 %all-gather.8.cloned.1.call-done = bf16[1024,2048]{1,0:T(8,128)(2,1)} async-done(((bf16[256,2048]{1,0:T(8,128)(2,1)}), bf16[1024,2048]{1,0:T(8,128)(2,1)}) %all-gather.8.cloned.1.call-update) | async-done | bytes 4194320 | tf_op jit(solution)/shard_map/all_gather | solution.py:121
  66.3 13.6 convolution_convert_fusion
  118.1 60.6 %all-to-all-done = bf16[4,1,259,2128]{3,2,1,0:T(8,128)(2,1)} async-done(((bf16[4,1,259,2128]{3,2,1,0:T(8,128)(2,1)}), bf16[4,1,259,2128]{3,2,1,0:T(8,128)(2,1)}, u32[]{:S(2)}, u32[]{:S(2)}) %all-to-all-start) | async-done | bytes 4409248 | tf_op jit(solution)/shard_map/all_to_all | solution.py:12
  241.5 43.3 %all-to-all-done.2 = bf16[4,256,1024]{1,2,0:T(8,128)(2,1)} async-done(((bf16[4,256,1024]{1,2,0:T(8,128)(2,1)}), bf16[4,256,1024]{1,2,0:T(8,128)(2,1)}, u32[]{:S(2)}, u32[]{:S(2)}) %all-to-all-start.2) | async-done | bytes 2097184 | tf_op jit(solution)/shard_map/all_to_all | solution.py:209
  306.5 32.7 %all-gather.12.cloned.1.call-done = f32[256,64,128]{2,1,0:T(8,128)} async-done(((f32[64,64,128]{2,1,0:T(8,128)}), f32[256,64,128]{2,1,0:T(8,128)}) %all-gather.12.cloned.1.call-update) | async-done | bytes 8388624 | tf_op jit(solution)/shard_map/all_gather | solution.py:18
  352.3 23.6 %multiply_reduce_fusion.11 = (f32[256]{0:T(256)S(1)}, f32[256,64,64]{0,2,1:T(8,128)S(1)}, f32[256,64,64]{0,2,1:T(8,128)}) fusion(f32[256,64,64]{0,2,1:T(8,128)} %bitcast.317, f32[256,64,64]{0,2,1:T(8,128)S(1)} %bitcast.305, f32[64]{0:T(128)S(1)} %copy-done.73, f32[256,64,64]{0,2,1:T(8,128)S(1)} %fusion.107, f32[256,64,64]{0,2,1:T(8,128)} %fusion.99, ...), kind=kOutput, calls=%fused_computation.90 | convolution fusion | flops 3251633920 | bytes 25691392 | tf_op jit(solution)/shard_map/jvp(tsh,shp->thp)/dot_general | solution.py:50
  427.3 26.2 %fusion.10 = (f32[256,64]{0,1:T(8,128)S(1)}, f32[256,64]{0,1:T(8,128)S(1)}, f32[256,64]{0,1:T(8,128)}, f32[256,256]{1,0:T(8,128)S(1)}) fusion(f32[256,64]{0,1:T(8,128)S(1)} %copy-done.43, f32[256,256]{1,0:T(8,128)S(1)} %copy-done.23, f32[256,64]{0,1:T(8,128)S(1)} %bitcast_bitcast_fusion.1, pred[256,256]{1,0:T(8,128)(4,1)S(1)} %fusion.102, ...), kind=kOutput, calls=%fused_computation.18 | convolution fusion | flops 3275636736 | bytes 9306112 | tf_op jit(solution)/shard_map/transpose(jvp(tsh,shp->thp))/dot_general | solution.py:50
  454.7 24.7 %all-gather.14.cloned.1.call-done = f32[256,64,128]{2,1,0:T(8,128)} async-done(((f32[64,64,128]{2,1,0:T(8,128)}), f32[256,64,128]{2,1,0:T(8,128)}) %all-gather.14.cloned.1.call-update) | async-done | bytes 8388624 | tf_op jit(solution)/shard_map/all_gather | solution.py:18
  479.5 14.9 %while.32 = (s32[]{:T(128)}, f32[64,64,128]{2,1,0:T(8,128)}, s32[]{:T(128)}, f32[4,64]{1,0:T(4,128)S(1)}, f32[4,64,64,128]{3,2,1,0:T(8,128)}, /*index=5*/s32[]{:T(128)}, s32[]{:T(128)}, s32[]{:T(128)}, s32[]{:T(128)}) while((s32[]{:T(128)}, f32[64,64,128]{2,1,0:T(8,128)}, s32[]{:T(128)}, f32[4,64]{1,0:T(4,128)S(1)}, ...), condition=%wide.region_12.13_spmd.clone, body=%wide.region_11.12_spmd.clone.sunk | while | flops 2097160 | bytes 6292391 | solution.py:31
  511.2 15.7 %fusion.31 = f32[256,64,64]{0,2,1:T(8,128)} fusion(f32[256,64,64]{0,2,1:T(8,128)S(1)} %get-tuple-element.503, f32[256,64,64]{0,2,1:T(8,128)S(1)} %copy-done.7, f32[64]{0:T(128)S(1)} %copy-done.73, f32[256,64]{0,1:T(8,128)S(1)} %get-tuple-element.490, f32[256,64]{0,1:T(8,128)S(1)} %copy-done.43, f32[256,256]{1,0:T(8,128)S(1)} %copy-done.24, ...), kind=kOutput, calls=%fused_computation.61 | convolution fusion | flops 3242196992 | bytes 13107456 | tf_op jit(solution)/shard_map/transpose(jvp(tsh,shp->thp))/dot_general | solution.py:50
  532.9 12.2 multiply_reduce_fusion.4
  573.1 15.8 %concatenate.35 = f32[259,4,2128]{2,1,0:T(4,128)} concatenate(f32[259,4,1024]{2,1,0:T(4,128)} %copy.282, f32[259,4,1024]{2,1,0:T(4,128)} %reshape.444, f32[259,4,32]{2,1,0:T(4,128)S(1)} %copy.283, f32[259,4,32]{2,1,0:T(4,128)S(1)} %copy.284, f32[259,4,16]{2,1,0:T(4,128)S(1)} %copy.285), dimensions={2} | concatenate | bytes 17636864 | tf_op jit(solution)/shard_map/concatenate | solution.py:246
  600.3 27.3 %copy.286 = f32[1,259,8512]{1,0,2:T(1,128)} copy(f32[1,259,8512]{2,1,0:T(8,128)} %reshape.453) | data formatting | bytes 17636864 | tf_op jit(solution)/shard_map/reshape | solution.py:246
  635.4 140.7 %all-to-all-done.3 = f32[1,259,8512]{1,0,2:T(1,128)} async-done(((f32[1,259,8512]{1,0,2:T(1,128)}), f32[1,259,8512]{1,0,2:T(1,128)}, u32[]{:S(2)}, u32[]{:S(2)}) %all-to-all-start.3) | async-done | bytes 8818464 | tf_op jit(solution)/shard_map/all_to_all | solution.py:249
  803.2 22.9 %scatter-add.4 = f32[4,256,2128]{1,2,0:T(8,128)} dynamic-update-slice(f32[4,256,2128]{1,2,0:T(8,128)} %copy-done.8, f32[3,3,2128]{1,2,0:T(8,128)S(1)} %add_select_fusion, s32[]{:T(128)} %bitcast.54, s32[]{:T(128)} %bitcast.55, s32[]{:T(128)} %constant.140.clone.1) | dynamic-update-slice | bytes 153220 | tf_op jit(solution)/shard_map/scatter-add | solution.py:251
  838.4 15.7 %fusion.155 = f32[1024,2048]{1,0:T(8,128)} fusion(bf16[1024,2128]{1,0:T(8,128)(2,1)} %bitcast.325, bf16[2048,2128]{1,0:T(8,128)(2,1)} %concatenate.29), kind=kOutput, calls=%fused_computation.251 | convolution fusion | flops 8925478912 | bytes 21463040 | tf_op jit(solution)/shard_map/dot_general | solution.py:254
  858.5 49.7 %all_to_all.52 = bf16[256,4,1024]{0,2,1:T(8,128)(2,1)S(1)} all-to-all(bf16[256,4,1024]{0,2,1:T(8,128)(2,1)S(1)} %fusion.48), channel_id=1, replica_groups=mesh['dp'=8,'tp'=4] {'tp'}, dimensions={1} | all-to-all | bytes 4194304 | tf_op jit(solution)/shard_map/all_to_all | solution.py:197
  932.0 12.9 fusion.156
  944.9 16.0 %pad_maximum_fusion = f32[2048,3152]{0,1:T(8,128)} fusion(f32[2048,1024]{0,1:T(8,128)} %convolution_bitcast_fusion, f32[2048,2128]{0,1:T(8,128)S(1)} %fusion.156), kind=kLoop, calls=%fused_computation.6 | loop fusion | flops 6455296 | bytes 51642368 | tf_op jit(solution)/shard_map/concatenate | solution.py:268
  966.4 41.9 %all-reduce.16 = (f32[2048]{0:T(1024)}, f32[4352]{0:T(1024)}, f32[64]{0:T(128)}, f32[64]{0:T(128)}, f32[64]{0:T(128)}, /*index=5*/f32[4096]{0:T(1024)}) all-reduce(f32[2048]{0:T(1024)S(1)} %get-tuple-element.425, f32[4352]{0:T(1024)S(1)} %copy-done.32, f32[64]{0:T(128)S(1)} %get-tuple-element.461, ...), channel_id=1, replica_groups=mesh['dp'=8,'tp'=4] {'dp','tp'}, use_global_device_ids=true, to_apply=%region_30.31 | all-reduce | flops 10688 | bytes 85504 | tf_op jit(solution)/shard_map/psum | solution.py:287
  1008.3 46.4 %reduce-scatter.4.cloned.1.call-done = f32[256,2048]{1,0:T(8,128)} async-done(((f32[1024,2048]{1,0:T(8,128)}), f32[256,2048]{1,0:T(8,128)}) %reduce-scatter.4.cloned.1.call-update) | async-done | bytes 2097168 | tf_op jit(solution)/shard_map/reduce_scatter | solution.py:198
  1059.0 249.3 %reduce-scatter.8.cloned.1.call-done = f32[256,3152]{0,1:T(8,128)} async-done(((f32[2048,3152]{0,1:T(8,128)}), f32[256,3152]{0,1:T(8,128)}) %reduce-scatter.8.cloned.1.call-update) | async-done | bytes 3227664 | tf_op jit(solution)/shard_map/reduce_scatter | solution.py:267
  1316.7 118.6 %all-reduce.19.cloned.1.call-done = f32[4352,4]{0,1:T(4,128)} async-done(((f32[4352,4]{0,1:T(4,128)}), f32[4352,4]{0,1:T(4,128)}) %all-reduce.19.cloned.1.call-update) | async-done | bytes 69648 | tf_op jit(solution)/shard_map/psum | solution.py:287
  (318 shorter events, 371.5 us)
Async XLA Ops:
  7.2 59.1 %all-gather.8.cloned.1.call-start = ((), (), s32[]{:S(2)}) async-start(), calls=%async_computation.7 | async-start | bytes 5242880 | tf_op jit(solution)/shard_map/all_gather | solution.py:121
  106.7 72.0 %all-to-all-start = ((bf16[4,1,259,2128]{3,2,1,0:T(8,128)(2,1)}), bf16[4,1,259,2128]{3,2,1,0:T(8,128)(2,1)}, u32[]{:S(2)}, u32[]{:S(2)}) async-start(bf16[4,1,259,2128]{3,2,1,0:T(8,128)(2,1)} %pad_maximum_fusion.1), calls=%async_computation | async-start | bytes 9191424 | tf_op jit(solution)/shard_map/all_to_all | solution.py:12
  111.8 114.3 %all-gather.10.cloned.1.call-start = ((), (), s32[]{:S(2)}) async-start(), calls=%async_computation.9 | async-start | bytes 5242880 | tf_op jit(solution)/shard_map/all_gather | solution.py:205
  112.5 226.7 %all-gather.12.cloned.1.call-start = ((), (), s32[]{:S(2)}) async-start(), calls=%async_computation.13 | async-start | bytes 10485760 | tf_op jit(solution)/shard_map/all_gather | solution.py:18
  113.1 80.9 %copy-start.68 = (f32[64]{0:T(128)}, f32[64]{0:T(128)S(1)}, u32[]{:S(2)}) copy-start(f32[64]{0:T(128)S(1)} %exp.58) | copy-start | bytes 772
  113.4 73.5 %copy-start.45 = (s32[259]{0:T(512)}, s32[259]{0:T(512)S(1)}, u32[]{:S(2)}) copy-start(s32[259]{0:T(512)S(1)} %convert_reduce_fusion) | copy-start | bytes 3112
  194.1 24.8 %copy-start.20 = (bf16[256,4,16]{0,2,1:T(8,128)(2,1)}, bf16[256,4,16]{0,2,1:T(8,128)(2,1)S(1)}, u32[]{:S(2)}) copy-start(bf16[256,4,16]{0,2,1:T(8,128)(2,1)S(1)} %slice.224) | copy-start | bytes 98308
  219.0 133.2 %copy-start.42 = (f32[256,64]{0,1:T(8,128)}, f32[256,64]{0,1:T(8,128)S(1)}, u32[]{:S(2)}) copy-start(f32[256,64]{0,1:T(8,128)S(1)} %get-tuple-element.491) | copy-start | bytes 196612
  236.7 48.2 %all-to-all-start.2 = ((bf16[4,256,1024]{1,2,0:T(8,128)(2,1)}), bf16[4,256,1024]{1,2,0:T(8,128)(2,1)}, u32[]{:S(2)}, u32[]{:S(2)}) async-start(bf16[4,256,1024]{1,2,0:T(8,128)(2,1)} %copy.273), calls=%async_computation.3 | async-start | bytes 4194304 | tf_op jit(solution)/shard_map/all_to_all | solution.py:209
  241.2 238.3 %all-gather.14.cloned.1.call-start = ((), (), s32[]{:S(2)}) async-start(), calls=%async_computation.14 | async-start | bytes 10485760 | tf_op jit(solution)/shard_map/all_gather | solution.py:18
  241.5 185.7 %copy-start.40 = (pred[256,256]{1,0:T(8,128)(4,1)}, pred[256,256]{1,0:T(8,128)(4,1)S(1)}, u32[]{:S(2)}) copy-start(pred[256,256]{1,0:T(8,128)(4,1)S(1)} %fusion.102) | copy-start | bytes 196612
  296.4 55.8 %copy-start.22 = (f32[256,256]{1,0:T(8,128)}, f32[256,256]{1,0:T(8,128)S(1)}, u32[]{:S(2)}) copy-start(f32[256,256]{1,0:T(8,128)S(1)} %fusion.113) | copy-start | bytes 786436
  352.2 23.7 %copy-start.16 = (f32[256,64,64]{0,2,1:T(8,128)}, f32[256,64,64]{0,2,1:T(8,128)S(1)}, u32[]{:S(2)}) copy-start(f32[256,64,64]{0,2,1:T(8,128)S(1)} %fusion.107) | copy-start | bytes 12582916
  352.2 23.6 %copy-start.11 = (f32[4,256,1024]{1,2,0:T(8,128)S(1)}, f32[4,256,1024]{1,2,0:T(8,128)}, u32[]{:S(2)}) copy-start(f32[4,256,1024]{1,2,0:T(8,128)} %convert_element_type.132) | copy-start | bytes 12582916
  375.9 18.6 %copy-start.47 = (f32[256]{0:T(256)}, f32[256]{0:T(256)S(1)}, u32[]{:S(2)}) copy-start(f32[256]{0:T(256)S(1)} %fusion.139) | copy-start | bytes 3076
  494.3 9.9 copy-start.4
  550.1 10.6 copy-start.44
  550.2 10.6 copy-start.69
  627.6 148.5 %all-to-all-start.3 = ((f32[1,259,8512]{1,0,2:T(1,128)}), f32[1,259,8512]{1,0,2:T(1,128)}, u32[]{:S(2)}, u32[]{:S(2)}) async-start(f32[1,259,8512]{1,0,2:T(1,128)} %copy.286), calls=%async_computation.4 | async-start | bytes 26148864 | tf_op jit(solution)/shard_map/all_to_all | solution.py:249
  634.0 329.9 %reduce-scatter.6.cloned.1.call-start = ((), (), s32[]{:S(2)}) async-start(), calls=%async_computation.10 | async-start | bytes 10485760 | tf_op jit(solution)/shard_map/reduce_scatter | solution.py:253
  854.2 200.5 %reduce-scatter.4.cloned.1.call-start = ((), (), s32[]{:S(2)}) async-start(), calls=%async_computation.8 | async-start | bytes 10485760 | tf_op jit(solution)/shard_map/reduce_scatter | solution.py:198
  921.3 387.0 %reduce-scatter.8.cloned.1.call-start = ((), (), s32[]{:S(2)}) async-start(), calls=%async_computation.11 | async-start | bytes 29048832 | tf_op jit(solution)/shard_map/reduce_scatter | solution.py:267
  961.1 474.2 %all-reduce.19.cloned.1.call-start = ((), (), s32[]{:S(2)}) async-start(), calls=%async_computation.12 | async-start | bytes 139264 | tf_op jit(solution)/shard_map/psum | solution.py:287
  964.0 90.7 %copy-start.18 = (f32[256,2048]{1,0:T(8,128)S(1)}, f32[256,2048]{1,0:T(8,128)}, u32[]{:S(2)}) copy-start(f32[256,2048]{1,0:T(8,128)} %reduce-scatter.6.cloned.1.call-done) | copy-start | bytes 6291460
  (63 other events, 266.6 us)
Sparse Core Ops, SparseCore 0:
  11.5 54.7 all-gather.7
  114.4 83.3 all-gather.9
  226.2 113.0 all-gather.11
  391.8 87.6 all-gather.13
  854.3 109.6 reduce-scatter.5
  967.2 87.4 reduce-scatter.3
  1057.1 251.1 reduce-scatter.7
  1315.4 119.8 all-reduce.18
